TPU v7x, 32 devices: a whole 2x2x4 slice. The times are simulated.
32 devices in a mesh: grp: 2 (over y), seq: 4 (over z), fsdp: 2 (over x), chan: 2 (over core).
Axes of the slice: x: 2, y: 2, z: 4, core: 2. Of those that a mesh axis runs over, the one named last changes fastest.
Arguments:
- tokens: bfloat16 [2048, 4096], P(('grp', 'seq', 'fsdp'), 'chan'), parts along dimension 0, may hold values from -6 to 6
- proj_weight: bfloat16 [4096, 3, 512], P('fsdp', None, 'chan'), may hold values from -0.09375 to 0.09375
- short_weight: float32 [3, 3, 512], P(None, None, 'chan'), may hold values from -3 to 3
- skip_gain: float32 [512], P('chan'), may hold values from -4 to 4
- filter_taps: bfloat16 [1024, 512], P(('seq', 'fsdp'), 'chan'), may hold values from -0.1875 to 0.1875
Outputs:
- mixed_out: bfloat16 [2048, 512], P(('grp', 'seq', 'fsdp'), 'chan'), parts along dimension 0
There are 2 independent parts, one for each index of `grp`. A program takes and returns all parts, laid end to end along the dimension named above; an argument that names none is the same for every part. Nothing has to cross between parts.
All inputs are finite; a program needn't handle non-finite values.
Results may differ from a plain program's by a relative error of at most 0.009.
Values may be sent and summed in bfloat16 or wider, within the bound.
A program may use at most 64 MiB of HBM per device.

v0:
```python
import math

import jax
import jax.numpy as jnp
from jax import lax
from jax.sharding import PartitionSpec as P


def shifted(value, axis, steps):
    count = lax.axis_size(axis)
    initial, last = (max(0, -steps), min(count, count - steps))
    return lax.ppermute(value, axis, [(source, source + steps) for source in range(initial, last)])


def index_grid(row_count, col_count):
    return (
        lax.broadcasted_iota(jnp.int32, (row_count, col_count), 0),
        lax.broadcasted_iota(jnp.int32, (row_count, col_count), 1),
    )


def phase_pair(row_ids, col_ids, period):
    wrapped = row_ids * col_ids % period
    phase = wrapped.astype(jnp.float32) * (2.0 * math.pi / period)
    return (jnp.cos(phase), jnp.sin(phase))


def multiply(real_x, imag_x):
    sig_real = real_x[0].astype(jnp.float32)
    sig_imag = imag_x[0].astype(jnp.float32)
    tap_real = real_x[1].astype(jnp.float32)
    tap_imag = imag_x[1].astype(jnp.float32)
    real_z = (sig_real * tap_real - sig_imag * tap_imag).astype(jnp.bfloat16)
    imag_z = (sig_real * tap_imag + sig_imag * tap_real).astype(jnp.bfloat16)
    return (real_z, imag_z)


def spread(stacked, groups, inner_shape):
    shaped = stacked.reshape((2, groups, 1) + inner_shape)
    moved = lax.all_to_all(shaped, ("seq", "fsdp"), split_axis=1, concat_axis=2, tiled=True)
    return moved.reshape((2, groups) + inner_shape)


def per_device(tokens, proj_weight, short_weight, skip_gain, filter_taps):
    whole = lax.all_gather(tokens, "chan", axis=1, tiled=True)
    row_count = whole.shape[0]
    width = proj_weight.shape[2]
    flat_width = 3 * width
    piece = lax.all_gather(proj_weight, "fsdp", axis=0, tiled=True)
    summed = jnp.dot(
        whole, piece.reshape(piece.shape[0], flat_width), preferred_element_type=jnp.float32
    )
    projected = summed.astype(jnp.bfloat16).reshape(row_count, 3, width)
    earlier = shifted(projected[row_count - 2 :], ("seq", "fsdp"), 1)
    extended = jnp.concatenate([earlier, projected], axis=0).astype(jnp.float32)
    mixed = (
        short_weight[0] * extended[2:]
        + short_weight[1] * extended[1:-1]
        + short_weight[2] * extended[:-2]
    )
    query = mixed[:, 0]
    product = (mixed[:, 1] * mixed[:, 2]).astype(jnp.bfloat16)
    groups = lax.axis_size(("seq", "fsdp"))
    position = lax.axis_index(("seq", "fsdp"))
    period_rows = 2 * groups
    length = period_rows * row_count
    scale = 1.0 / length
    bin_ids, tap_ids = index_grid(period_rows, groups)
    first_cos, first_sin = phase_pair(bin_ids, tap_ids, period_rows)
    first_cos = first_cos.astype(jnp.bfloat16)
    first_sin = first_sin.astype(jnp.bfloat16)
    col_ids, freq_ids = index_grid(row_count, row_count)
    last_cos, last_sin = phase_pair(col_ids, freq_ids, row_count)
    last_cos = last_cos.astype(jnp.bfloat16)
    last_sin = last_sin.astype(jnp.bfloat16)
    stacked = jnp.stack([product, filter_taps])
    f32 = jnp.float32
    per_dev = row_count // groups
    per_bins = period_rows // groups
    arrived = spread(stacked.reshape(2, groups, per_dev, width), groups, (per_dev, width))
    real_a = jnp.einsum("qp,kpmc->kqmc", first_cos, arrived, preferred_element_type=f32)
    imag_a = -jnp.einsum("qp,kpmc->kqmc", first_sin, arrived, preferred_element_type=f32)
    row_ids, mid_ids = index_grid(period_rows, per_dev)
    twist_cos, twist_sin = phase_pair(row_ids, mid_ids + position * per_dev, length)
    twist_cos = twist_cos[:, :, None]
    twist_sin = twist_sin[:, :, None]
    real_b = (real_a * twist_cos + imag_a * twist_sin).astype(jnp.bfloat16)
    imag_b = (imag_a * twist_cos - real_a * twist_sin).astype(jnp.bfloat16)
    outgoing = jnp.stack([real_b, imag_b]).reshape(2, 2, groups, per_bins, 1, per_dev, width)
    turned = lax.all_to_all(outgoing, ("seq", "fsdp"), split_axis=2, concat_axis=4, tiled=True)
    turned = turned.reshape(2, 2, per_bins, row_count, width)
    real_b = turned[0]
    imag_b = turned[1]
    real_x = (
        jnp.einsum("kqmc,mr->kqrc", real_b, last_cos, preferred_element_type=f32)
        + jnp.einsum("kqmc,mr->kqrc", imag_b, last_sin, preferred_element_type=f32)
    ).astype(jnp.bfloat16)
    imag_x = (
        jnp.einsum("kqmc,mr->kqrc", imag_b, last_cos, preferred_element_type=f32)
        - jnp.einsum("kqmc,mr->kqrc", real_b, last_sin, preferred_element_type=f32)
    ).astype(jnp.bfloat16)
    real_z, imag_z = multiply(real_x, imag_x)
    real_v = jnp.einsum("qrc,mr->qmc", real_z, last_cos, preferred_element_type=f32) - jnp.einsum(
        "qrc,mr->qmc", imag_z, last_sin, preferred_element_type=f32
    )
    imag_v = jnp.einsum("qrc,mr->qmc", imag_z, last_cos, preferred_element_type=f32) + jnp.einsum(
        "qrc,mr->qmc", real_z, last_sin, preferred_element_type=f32
    )
    row_ids, mid_ids = index_grid(per_bins, row_count)
    twist_cos, twist_sin = phase_pair(row_ids + position * per_bins, mid_ids, length)
    twist_cos = twist_cos[:, :, None]
    twist_sin = twist_sin[:, :, None]
    real_w = (real_v * twist_cos - imag_v * twist_sin).astype(jnp.bfloat16)
    imag_w = (imag_v * twist_cos + real_v * twist_sin).astype(jnp.bfloat16)
    backward = jnp.stack([real_w, imag_w]).reshape(2, 1, per_bins, groups, per_dev, width)
    returned = lax.all_to_all(backward, ("seq", "fsdp"), split_axis=3, concat_axis=1, tiled=True)
    returned = returned.reshape(2, period_rows, per_dev, width)
    conv_rows = jnp.einsum(
        "qp,qmc->pmc", first_cos, returned[0], preferred_element_type=f32
    ) - jnp.einsum("qp,qmc->pmc", first_sin, returned[1], preferred_element_type=f32)
    conv_rows = (conv_rows * scale).astype(jnp.bfloat16)
    homed = lax.all_to_all(
        conv_rows.reshape(groups, 1, per_dev, width),
        ("seq", "fsdp"),
        split_axis=0,
        concat_axis=1,
        tiled=True,
    )
    conv = homed.reshape(row_count, width)
    result = query * (conv.astype(jnp.float32) + skip_gain * product.astype(jnp.float32))
    return result.astype(jnp.bfloat16)


def solution(mesh):
    in_specs = (
        P(("grp", "seq", "fsdp"), "chan"),
        P("fsdp", None, "chan"),
        P(None, None, "chan"),
        P("chan"),
        P(("seq", "fsdp"), "chan"),
    )
    out_specs = P(("grp", "seq", "fsdp"), "chan")
    return jax.shard_map(
        per_device, mesh=mesh, in_specs=in_specs, out_specs=out_specs, check_vma=False
    )
```

profile of v0, /device:TPU:0, one launch (start us, length us, event | category | flops | bytes accessed | tf_op | source)
XLA Modules:
  0.0 182.0 jit_solution(7906080105272334590)
XLA Ops:
  6.5 0.0 all-gather.3.cloned.1.call-start
  6.5 0.7 all-gather.3.cloned.1.call-update
  7.3 0.0 all-gather.5.cloned.1.call-start
  7.3 4.7 %copy.33 = bf16[2048,3,256]{0,2,1:T(8,128)(2,1)} copy(bf16[2048,3,256]{2,0,1:T(8,128)(2,1)} %param.6) | data formatting | bytes 6291456 | tf_op args[1]
  12.0 0.0 copy-start.1
  12.0 0.0 all-gather.5.cloned.1.call-update
  12.0 0.0 copy-start
  12.1 8.6 %all-gather.3.cloned.1.call-done = bf16[128,4096]{1,0:T(8,128)(2,1)} async-done(((bf16[128,2048]{1,0:T(8,128)(2,1)}), bf16[128,4096]{1,0:T(8,128)(2,1)}) %all-gather.3.cloned.1.call-update) | async-done | bytes 1048592 | tf_op jit(solution)/shard_map/all_gather | solution.py:45
  20.7 83.1 %all-gather.5.cloned.1.call-done = bf16[4096,3,256]{0,2,1:T(8,128)(2,1)} async-done(((bf16[2048,3,256]{0,2,1:T(8,128)(2,1)}), bf16[4096,3,256]{0,2,1:T(8,128)(2,1)}) %all-gather.5.cloned.1.call-update) | async-done | bytes 6291472 | tf_op jit(solution)/shard_map/all_gather | solution.py:49
  103.8 5.3 %convolution_convert_fusion = bf16[128,768]{1,0:T(8,128)(2,1)S(1)} fusion(bf16[128,4096]{1,0:T(8,128)(2,1)} %all-gather.3.cloned.1.call-done, bf16[4096,768]{0,1:T(8,128)(2,1)} %bitcast.121), kind=kOutput, calls=%fused_computation.7 | convolution fusion | flops 805404672 | bytes 7536640 | tf_op jit(solution)/shard_map/dot_general | solution.py:50
  109.2 2.2 %collective-permute-start = (bf16[2,3,256]{2,1,0:T(4,128)(2,1)S(1)}, bf16[2,3,256]{2,1,0:T(4,128)(2,1)S(1)}, u32[]{:S(2)}, u32[]{:S(2)}) collective-permute-start(bf16[2,3,256]{2,1,0:T(4,128)(2,1)S(1)} %slice.63), channel_id=1, source_target_pairs={{0,2},{2,4},{4,6},{6,8},{8,10},{10,12},{12,14},{1,3},{3,5},{5,7},{... | collective-permute-start | bytes 9224 | tf_op jit(solution)/shard_map/ppermute | solution.py:12
  111.4 0.0 copy-done.1
  111.4 0.2 copy.34
  111.6 1.1 collective-permute-done
  112.7 0.2 copy.35
  112.9 0.2 maximum_convert_fusion
  113.1 0.6 fusion.10
  113.7 0.1 copy.36
  113.8 0.0 copy-done
  113.8 0.7 copy.37
  114.5 7.5 %all-to-all-start = ((bf16[2,8,1,16,256]{4,3,0,2,1:T(8,128)(2,1)}), bf16[2,8,1,16,256]{4,3,0,2,1:T(8,128)(2,1)S(1)}, u32[]{:S(2)}, u32[]{:S(2)}) async-start(bf16[2,8,1,16,256]{4,3,0,2,1:T(8,128)(2,1)} %copy.37), calls=%async_computation | async-start | bytes 262144 | tf_op jit(solution)/shard_map/all_to_all | solution.py:40
  121.9 0.1 fusion.57
  122.1 7.2 %all-to-all-done = bf16[2,8,1,16,256]{4,3,0,2,1:T(8,128)(2,1)S(1)} async-done(((bf16[2,8,1,16,256]{4,3,0,2,1:T(8,128)(2,1)}), bf16[2,8,1,16,256]{4,3,0,2,1:T(8,128)(2,1)S(1)}, u32[]{:S(2)}, u32[]{:S(2)}) %all-to-all-start) | async-done | bytes 131104 | tf_op jit(solution)/shard_map/all_to_all | solution.py:40
  129.3 0.3 convolution_bitcast_fusion
  129.6 0.4 add_convert_fusion
  130.0 0.1 stack.27
  130.1 0.1 stack.28
  130.2 0.7 pad_maximum_fusion
  131.0 1.4 copy.62
  132.4 3.5 %all-to-all-start.1 = ((bf16[2,2,8,2,1,16,256]{6,3,5,1,4,0,2:T(2,128)(2,1)}), bf16[2,2,8,2,1,16,256]{6,3,5,1,4,0,2:T(2,128)(2,1)S(1)}, u32[]{:S(2)}, u32[]{:S(2)}) async-start(bf16[2,2,8,2,1,16,256]{6,3,5,1,4,0,2:T(2,128)(2,1)} %copy.62), calls=%async_computation.1 | async-start | bytes 1048576 | tf_op jit(solution)/shard_map/all_to_all | solution.py:90
  135.9 0.0 copy-start.2
  135.9 0.1 fusion.69
  136.0 12.0 %all-to-all-done.1 = bf16[2,2,8,2,1,16,256]{6,3,5,1,4,0,2:T(2,128)(2,1)S(1)} async-done(((bf16[2,2,8,2,1,16,256]{6,3,5,1,4,0,2:T(2,128)(2,1)}), bf16[2,2,8,2,1,16,256]{6,3,5,1,4,0,2:T(2,128)(2,1)S(1)}, u32[]{:S(2)}, u32[]{:S(2)}) %all-to-all-start.1) | async-done | bytes 524320 | tf_op jit(solution)/shard_map/all_to_all | solution.py:90
  148.0 0.6 fusion.118
  148.6 0.5 fusion.41
  149.1 0.5 fusion.39
  149.6 0.5 fusion.4
  150.1 0.5 fusion.3
  150.6 0.1 fusion.16
  150.7 0.4 fusion.45
  151.1 0.4 fusion.43
  151.5 0.4 fusion.6
  151.9 0.4 subtract_convert_fusion.1
  152.3 11.7 %all_to_all.48 = bf16[2,1,2,8,16,256]{5,4,2,1,0,3:T(8,128)(2,1)S(1)} all-to-all(bf16[2,1,2,8,16,256]{5,4,2,1,0,3:T(8,128)(2,1)S(1)} %copy.66), channel_id=1, replica_groups=mesh['grp'=2,'seq'=4,'fsdp'=2,'chan'=2] {'seq','fsdp'}, dimensions={3} | all-to-all | bytes 524288 | tf_op jit(solution)/shard_map/all_to_all | solution.py:116
  164.0 0.2 fusion.23
  164.2 0.2 fusion.9
  164.5 9.7 %all_to_all.49 = bf16[8,1,16,256]{3,2,1,0:T(8,128)(2,1)S(1)} all-to-all(bf16[8,1,16,256]{3,2,1,0:T(8,128)(2,1)S(1)} %copy.51), channel_id=1, replica_groups=mesh['grp'=2,'seq'=4,'fsdp'=2,'chan'=2] {'seq','fsdp'}, dimensions={0} | all-to-all | bytes 131072 | tf_op jit(solution)/shard_map/all_to_all | solution.py:122
  174.2 0.1 copy.53
  174.3 0.0 copy-done.2
  174.3 0.1 fusion.20
  174.4 0.7 copy.54
  (14 shorter events, 0.2 us)
Async XLA Ops:
  6.5 14.1 %all-gather.3.cloned.1.call-start = ((), (), s32[]{:S(2)}) async-start(), calls=%async_computation.4 | async-start | bytes 1572864 | tf_op jit(solution)/shard_map/all_gather | solution.py:45
  7.3 96.5 %all-gather.5.cloned.1.call-start = ((), (), s32[]{:S(2)}) async-start(), calls=%async_computation.5 | async-start | bytes 9437184 | tf_op jit(solution)/shard_map/all_gather | solution.py:49
  12.0 99.4 %copy-start.1 = (f32[3,3,256]{2,1,0:T(4,128)S(1)}, f32[3,3,256]{2,1,0:T(4,128)}, u32[]{:S(2)}) copy-start(f32[3,3,256]{2,1,0:T(4,128)} %param.7) | copy-start | bytes 27652
  12.0 101.7 %copy-start = (bf16[128,256]{1,0:T(8,128)(2,1)S(1)}, bf16[128,256]{1,0:T(8,128)(2,1)}, u32[]{:S(2)}) copy-start(bf16[128,256]{1,0:T(8,128)(2,1)} %param.9) | copy-start | bytes 196612
  109.2 3.5 %collective-permute-start = (bf16[2,3,256]{2,1,0:T(4,128)(2,1)S(1)}, bf16[2,3,256]{2,1,0:T(4,128)(2,1)S(1)}, u32[]{:S(2)}, u32[]{:S(2)}) collective-permute-start(bf16[2,3,256]{2,1,0:T(4,128)(2,1)S(1)} %slice.63), channel_id=1, source_target_pairs={{0,2},{2,4},{4,6},{6,8},{8,10},{10,12},{12,14},{1,3},{3,5},{5,7},{... | collective-permute-start | bytes 9224 | tf_op jit(solution)/shard_map/ppermute | solution.py:12
  114.5 14.8 %all-to-all-start = ((bf16[2,8,1,16,256]{4,3,0,2,1:T(8,128)(2,1)}), bf16[2,8,1,16,256]{4,3,0,2,1:T(8,128)(2,1)S(1)}, u32[]{:S(2)}, u32[]{:S(2)}) async-start(bf16[2,8,1,16,256]{4,3,0,2,1:T(8,128)(2,1)} %copy.37), calls=%async_computation | async-start | bytes 262144 | tf_op jit(solution)/shard_map/all_to_all | solution.py:40
  132.4 15.6 %all-to-all-start.1 = ((bf16[2,2,8,2,1,16,256]{6,3,5,1,4,0,2:T(2,128)(2,1)}), bf16[2,2,8,2,1,16,256]{6,3,5,1,4,0,2:T(2,128)(2,1)S(1)}, u32[]{:S(2)}, u32[]{:S(2)}) async-start(bf16[2,2,8,2,1,16,256]{6,3,5,1,4,0,2:T(2,128)(2,1)} %copy.62), calls=%async_computation.1 | async-start | bytes 1048576 | tf_op jit(solution)/shard_map/all_to_all | solution.py:90
  135.9 38.5 %copy-start.2 = (f32[256]{0:T(256)S(1)}, f32[256]{0:T(256)}, u32[]{:S(2)}) copy-start(f32[256]{0:T(256)} %param.8) | copy-start | bytes 3076
Sparse Core Ops, SparseCore 0:
  8.9 11.7 all-gather.2
  22.2 81.5 all-gather.4
where the time goes:
time: 182 us
  waiting for transfers between devices  113 us (62%)
  blocking collectives  21.4 us (12%)
  between operations  13.7 us (8%)
  starting transfers between devices  13.2 us (7%)
  matrix products  9.98 us (5%)
  local copies, waits for them, and re-layouts  8.96 us (5%)
  other arithmetic  2.03 us (1%)
    all_gather x1, waiting for transfers between devices, per_device(): piece = lax.all_gather(proj_weight, 'fsdp', axis=0, tiled=True)  83.1 us
    all_to_all x1, waiting for transfers between devices, per_device(): lax.all_to_all(outgoing, ('seq', 'fsdp'), split_axis=2, concat_axis=4, ti...  12 us
    all_to_all x1, blocking collectives, per_device(): lax.all_to_all(backward, ('seq', 'fsdp'), split_axis=3, concat_axis=1, ti...  11.7 us
    all_to_all x1, blocking collectives, per_device(): lax.all_to_all(conv_rows.reshape(groups, 1, per_dev, width), ('seq', 'fsd...  9.74 us
    all_gather x1, waiting for transfers between devices, per_device(): whole = lax.all_gather(tokens, 'chan', axis=1, tiled=True)  8.61 us
    all_to_all x1, starting transfers between devices, spread(): lax.all_to_all(shaped, ('seq', 'fsdp'), split_axis=1, concat_axis=2, tile...  7.46 us
    all_to_all x1, waiting for transfers between devices, spread(): lax.all_to_all(shaped, ('seq', 'fsdp'), split_axis=1, concat_axis=2, tile...  7.21 us
    dot_general x1, matrix products, per_device(): jnp.dot(whole, piece.reshape(piece.shape[0], flat_width), preferred_eleme...  5.33 us
  transfers between devices with their start and end apart: 5, of which 5 were waited for; matrix products, arithmetic and copies ran while one was open for 3% of the time, Pallas kernels for 0%

commit v1 on v0

v1 whole, which is shorter than its diff:
```python
import functools
import math

import jax
import jax.numpy as jnp
import ml_dtypes
import numpy as np
from jax import lax
from jax.experimental import pallas as pl
from jax.experimental.pallas import tpu as pltpu
from jax.sharding import PartitionSpec as P

MESH = pl.DeviceIdType.MESH
BF16 = jnp.bfloat16
F32 = jnp.float32
CHUNKS = 4


def phase_pair(rows, cols, period):
    wrapped = (np.arange(rows)[:, None] * np.arange(cols)[None, :]) % period
    phase = wrapped.astype(np.float32) * np.float32(2.0 * math.pi / period)
    return np.cos(phase), np.sin(phase)


def tables(groups, per, rows):
    bf = ml_dtypes.bfloat16
    bins = 2 * groups
    cos, sin = phase_pair(bins, groups, bins)
    eye = np.eye(per, dtype=np.float32)
    first = np.concatenate([np.kron(cos, eye), np.kron(-sin, eye)], axis=0).astype(bf)
    cos, sin = phase_pair(rows, rows, rows)
    ahead = np.block([[cos, -sin], [sin, cos]]).astype(bf)
    behind = np.block([[cos, sin], [-sin, cos]]).astype(bf)
    cos, sin = phase_pair(bins, rows, bins * rows)
    twist = np.stack([np.repeat(cos, per, axis=0), np.repeat(sin, per, axis=0)])
    last = np.ascontiguousarray(first.T)
    return first, last, ahead, behind, twist.astype(np.float32)


def kernel(
    sizes,
    tokens,
    weight,
    short,
    gain,
    taps,
    first_h,
    last_h,
    ahead_h,
    behind_h,
    twist_h,
    out,
    w,
    first,
    last,
    ahead,
    behind,
    twist,
    held,
    acc,
    psend,
    precv,
    hsend,
    hrecv,
    query,
    product,
    tsend,
    trecv,
    gsend,
    grecv,
    csend,
    crecv,
    tapspec,
    load_sem,
    tok_send,
    tok_recv,
    part_send,
    part_recv,
    halo_sem,
    a2a_send,
    a2a_recv,
):
    seq, fsdp, chan = sizes
    groups = seq * fsdp
    rows = tokens.shape[0]
    depth = weight.shape[1]
    width = weight.shape[2]
    per = width // groups
    bins = 2 * groups
    step = depth // CHUNKS
    share = fsdp // chan
    s = lax.axis_index("seq")
    f = lax.axis_index("fsdp")
    c = lax.axis_index("chan")
    me = s * fsdp + f

    loads = [
        pltpu.make_async_copy(source, target, load_sem.at[i])
        for i, (source, target) in enumerate(
            [
                (weight, w),
                (first_h, first),
                (last_h, last),
                (ahead_h, ahead),
                (behind_h, behind),
                (twist_h, twist),
            ]
        )
    ]
    for load in loads:
        load.start()

    barrier = pltpu.get_barrier_semaphore()
    everyone = groups * chan

    def greet(k, carry):
        other = lax.rem(me * chan + c + k, everyone)
        spot = other // chan
        pl.semaphore_signal(
            barrier,
            inc=1,
            device_id={"seq": spot // fsdp, "fsdp": spot % fsdp, "chan": other % chan},
            device_id_type=MESH,
        )
        return carry

    lax.fori_loop(1, everyone, greet, 0)
    pl.semaphore_wait(barrier, everyone - 1)

    def token_copy(i, cc, k):
        return pltpu.make_async_remote_copy(
            src_ref=tokens.at[:, pl.ds(i * depth + k * step, step)],
            dst_ref=held.at[f, k],
            send_sem=tok_send.at[i * chan + cc, k],
            recv_sem=tok_recv.at[f, k],
            device_id={"fsdp": c * share + i, "chan": cc},
            device_id_type=MESH,
        )

    def own_copy(i, k):
        return pltpu.make_async_copy(
            tokens.at[:, pl.ds(i * depth + k * step, step)], held.at[f, k], tok_recv.at[f, k]
        )

    for k in range(CHUNKS):
        for i in range(share):
            for cc in range(chan):
                is_self = jnp.logical_and(c * share + i == f, c == cc)

                @pl.when(jnp.logical_not(is_self))
                def _():
                    token_copy(i, cc, k).start()

                @pl.when(is_self)
                def _():
                    own_copy(i, k).start()

    def exchange_copy(which, source, target, k):
        other = lax.rem(me + k, groups)
        return pltpu.make_async_remote_copy(
            src_ref=source.at[other],
            dst_ref=target.at[me],
            send_sem=a2a_send.at[which, k],
            recv_sem=a2a_recv.at[which, k],
            device_id={"seq": other // fsdp, "fsdp": other % fsdp},
            device_id_type=MESH,
        )

    def exchange_start(which, source, target):
        def go(k, carry):
            exchange_copy(which, source, target, k).start()
            return carry

        lax.fori_loop(1, groups, go, 0)
        target[me] = source[me]

    def exchange_wait(which, source, target):
        def go(k, carry):
            copy = exchange_copy(which, source, target, k)
            copy.wait_send()
            copy.wait_recv()
            return carry

        lax.fori_loop(1, groups, go, 0)

    tsend[...] = jnp.transpose(taps[...].astype(F32)).astype(BF16).reshape(groups, per, rows)
    exchange_start(0, tsend, trecv)

    half = bins * per

    def spectrum(signal):
        a = jnp.dot(first[...], signal, preferred_element_type=F32)
        real_a, imag_a = a[:half], a[half:]
        real_b = (real_a * twist[0] + imag_a * twist[1]).astype(BF16)
        imag_b = (imag_a * twist[0] - real_a * twist[1]).astype(BF16)
        b = jnp.concatenate([real_b, imag_b], axis=1)
        return jnp.dot(b, ahead[...], preferred_element_type=F32).astype(BF16)

    for load in loads[1:]:
        load.wait()
    exchange_wait(0, tsend, trecv)
    tapspec[...] = spectrum(trecv[...].reshape(width, rows))
    loads[0].wait()

    def part_copy(d):
        other = lax.rem(f + d, fsdp)
        return pltpu.make_async_remote_copy(
            src_ref=psend.at[d - 1],
            dst_ref=precv.at[d - 1],
            send_sem=part_send.at[d - 1],
            recv_sem=part_recv.at[d - 1],
            device_id={"fsdp": other},
            device_id_type=MESH,
        )

    for d in range(1, fsdp + 1):
        spot = lax.rem(f + d, fsdp)
        for k in range(CHUNKS):
            pltpu.make_async_copy(held.at[spot, k], held.at[spot, k], tok_recv.at[spot, k]).wait()
            block = held[spot, k]
            for j in range(3):
                term = jnp.dot(
                    block, w[j, k * step : (k + 1) * step, :], preferred_element_type=F32
                )
                if k == 0:
                    acc[j] = term
                else:
                    acc[j] += term
        if d < fsdp:
            psend[d - 1] = acc[...].astype(BF16)
            part_copy(d).start()

    for d in range(1, fsdp):
        part_copy(d).wait_recv()
    total = acc[...]
    for d in range(1, fsdp):
        total = total + precv[d - 1].astype(F32)
    projected = total.astype(BF16).astype(F32)

    following = jnp.minimum(me + 1, groups - 1)
    halo = pltpu.make_async_remote_copy(
        src_ref=hsend,
        dst_ref=hrecv,
        send_sem=halo_sem.at[0],
        recv_sem=halo_sem.at[1],
        device_id={"seq": following // fsdp, "fsdp": following % fsdp},
        device_id_type=MESH,
    )
    hsend[...] = projected[:, rows - 8 :, :]

    @pl.when(me < groups - 1)
    def _():
        halo.start()

    @pl.when(me == 0)
    def _():
        hrecv[...] = jnp.zeros_like(hrecv)

    @pl.when(me > 0)
    def _():
        halo.wait_recv()

    row_ids = lax.broadcasted_iota(jnp.int32, (rows, width), 0)
    branches = []
    for j in range(3):
        now = projected[j]
        before = hrecv[j, 7:8, :]
        earlier = hrecv[j, 6:7, :]
        one = jnp.where(row_ids == 0, before, pltpu.roll(now, 1, 0))
        two = jnp.where(
            row_ids == 0, earlier, jnp.where(row_ids == 1, before, pltpu.roll(now, 2, 0))
        )
        branches.append(
            short[0, j : j + 1, :] * now
            + short[1, j : j + 1, :] * one
            + short[2, j : j + 1, :] * two
        )
    prod = (branches[1] * branches[2]).astype(BF16).astype(F32)
    gsend[...] = jnp.transpose(prod).astype(BF16).reshape(groups, per, rows)
    exchange_start(1, gsend, grecv)
    query[...] = branches[0]
    product[...] = prod * gain[...]
    exchange_wait(1, gsend, grecv)

    x = spectrum(grecv[...].reshape(width, rows)).astype(F32)
    t = tapspec[...].astype(F32)
    xr, xi = x[:, :rows], x[:, rows:]
    tr, ti = t[:, :rows], t[:, rows:]
    real_z = (xr * tr - xi * ti).astype(BF16)
    imag_z = (xr * ti + xi * tr).astype(BF16)
    z = jnp.concatenate([real_z, imag_z], axis=1)
    v = jnp.dot(z, behind[...], preferred_element_type=F32)
    vr, vi = v[:, :rows], v[:, rows:]
    real_w = (vr * twist[0] - vi * twist[1]).astype(BF16)
    imag_w = (vi * twist[0] + vr * twist[1]).astype(BF16)
    packed = jnp.concatenate([real_w, imag_w], axis=0)
    y = jnp.dot(last[...], packed, preferred_element_type=F32) * (1.0 / (bins * rows))
    csend[...] = y.astype(BF16).reshape(groups, per, rows)
    exchange_start(2, csend, crecv)
    exchange_wait(2, csend, crecv)
    conv = jnp.transpose(crecv[...].reshape(width, rows).astype(F32))
    out[...] = (query[...] * (conv + product[...])).astype(BF16)

    @pl.when(me < groups - 1)
    def _():
        halo.wait_send()

    for d in range(1, fsdp):
        part_copy(d).wait_send()
    for k in range(CHUNKS):
        for i in range(share):
            for cc in range(chan):
                is_self = jnp.logical_and(c * share + i == f, c == cc)

                @pl.when(jnp.logical_not(is_self))
                def _():
                    token_copy(i, cc, k).wait_send()


def per_device(sizes, tokens, proj_weight, short_weight, skip_gain, filter_taps):
    seq, fsdp, chan = sizes
    groups = seq * fsdp
    rows = tokens.shape[0]
    depth, branches, width = proj_weight.shape
    per = width // groups
    made = tables(groups, per, rows)
    dma = pltpu.SemaphoreType.DMA
    vmem = pl.BlockSpec(memory_space=pltpu.VMEM)
    anywhere = pl.BlockSpec(memory_space=pl.ANY)
    half = 2 * groups * per
    return pl.pallas_call(
        functools.partial(kernel, sizes),
        out_shape=jax.ShapeDtypeStruct((rows, width), BF16),
        in_specs=[anywhere, anywhere, vmem, vmem, vmem] + [anywhere] * 5,
        out_specs=vmem,
        scratch_shapes=[
            pltpu.VMEM((branches, depth, width), BF16),
            pltpu.VMEM(made[0].shape, BF16),
            pltpu.VMEM(made[1].shape, BF16),
            pltpu.VMEM(made[2].shape, BF16),
            pltpu.VMEM(made[3].shape, BF16),
            pltpu.VMEM(made[4].shape, F32),
            pltpu.VMEM((fsdp, CHUNKS, rows, depth // CHUNKS), BF16),
            pltpu.VMEM((branches, rows, width), F32),
            pltpu.VMEM((fsdp - 1, branches, rows, width), BF16),
            pltpu.VMEM((fsdp - 1, branches, rows, width), BF16),
            pltpu.VMEM((branches, 8, width), F32),
            pltpu.VMEM((branches, 8, width), F32),
            pltpu.VMEM((rows, width), F32),
            pltpu.VMEM((rows, width), F32),
        ]
        + [pltpu.VMEM((groups, per, rows), BF16)] * 6
        + [
            pltpu.VMEM((half, 2 * rows), BF16),
            dma((6,)),
            dma((fsdp, CHUNKS)),
            dma((fsdp, CHUNKS)),
            dma((fsdp - 1,)),
            dma((fsdp - 1,)),
            dma((2,)),
            dma((3, groups)),
            dma((3, groups)),
        ],
        compiler_params=pltpu.CompilerParams(
            collective_id=0, has_side_effects=True, vmem_limit_bytes=48 * 1024 * 1024
        ),
        name="hyena",
    )(
        tokens,
        jnp.transpose(proj_weight, (1, 0, 2)),
        short_weight,
        skip_gain.reshape(1, width),
        filter_taps,
        *[jnp.asarray(table) for table in made],
    )


def solution(mesh):
    sizes = (mesh.shape["seq"], mesh.shape["fsdp"], mesh.shape["chan"])
    in_specs = (
        P(("grp", "seq", "fsdp"), "chan"),
        P("fsdp", None, "chan"),
        P(None, None, "chan"),
        P("chan"),
        P(("seq", "fsdp"), "chan"),
    )
    out_specs = P(("grp", "seq", "fsdp"), "chan")
    return jax.shard_map(
        functools.partial(per_device, sizes),
        mesh=mesh,
        in_specs=in_specs,
        out_specs=out_specs,
        check_vma=False,
    )
```

time: 182 us -> 51.1 us (0.28)
  waiting for transfers between devices: 113 us -> 0 us
  Pallas kernels: 0 us -> 39.9 us
  blocking collectives: 21.4 us -> 0 us
  between operations: 13.7 us -> 0.02 us
  starting transfers between devices: 13.2 us -> 0 us
  matrix products: 9.98 us -> 0 us
  other arithmetic: 2.03 us -> 0 us
    all_gather x2 -> x0, waiting for transfers between devices: 91.7 us -> none  [the longest x1 83.1 us: per_device(): piece = lax.all_gather(proj_weight, 'fsdp', axis=0, tiled=True)]
    pallas_call x0 -> x1, Pallas kernels: none -> 39.9 us  [per_device(): pl.pallas_call(functools.partial(kernel, sizes), out_shape=jax.ShapeDtype...]
    all_to_all x2 -> x0, blocking collectives: 21.4 us -> none  [the longest x1 11.7 us: per_device(): lax.all_to_all(backward, ('seq', 'fsdp'), split_axis=3, concat_axis=1, ti...]
    all_to_all x2 -> x0, waiting for transfers between devices: 19.2 us -> none  [the longest x1 12 us: per_device(): lax.all_to_all(outgoing, ('seq', 'fsdp'), split_axis=2, concat_axis=4, ti...]
    all_to_all x2 -> x0, starting transfers between devices: 11 us -> none  [the longest x1 7.46 us: spread(): lax.all_to_all(shaped, ('seq', 'fsdp'), split_axis=1, concat_axis=2, tile...]
    dot_general x13 -> x0, matrix products: 9.98 us -> none  [the longest x1 5.33 us: per_device(): jnp.dot(whole, piece.reshape(piece.shape[0], flat_width), preferred_eleme...]
    unnamed x7 -> x21, local copies, waits for them, and re-layouts: 4.73 us -> 10.7 us
    another operation x5 -> x0, local copies, waits for them, and re-layouts: 2.24 us -> none  [the longest x3 1.57 us: per_device(): jnp.stack([real_b, imag_b])]
  transfers between devices with their start and end apart: 5 -> 0, of which waited for: 5 -> 0; matrix products, arithmetic and copies ran while one was open for 3% -> 0% of each run, Pallas kernels for 0% -> 0%
where the time goes in v1:
time: 51.1 us; the launch traced here: 50.7 us
  Pallas kernels  39.9 us (78%)
  local copies, waits for them, and re-layouts  10.7 us (21%)
    pallas_call x1, Pallas kernels, per_device(): pl.pallas_call(functools.partial(kernel, sizes), out_shape=jax.ShapeDtype...  39.9 us
    unnamed x21, local copies, waits for them, and re-layouts  10.7 us

profile of v1, /device:TPU:0, one launch (start us, length us, event | category | flops | bytes accessed | tf_op | source)
XLA Modules:
  0.0 50.7 jit_solution(17977646810055448610)
XLA Ops:
  0.0 0.0 copy-start
  0.0 1.9 %copy-done = bf16[2048,3,256]{2,0,1:T(8,128)(2,1)S(1)} copy-done((bf16[2048,3,256]{2,0,1:T(8,128)(2,1)S(1)}, bf16[2048,3,256]{2,0,1:T(8,128)(2,1)}, u32[]{:S(2)}) %copy-start) | copy-done | bytes 3145752
  1.9 0.0 copy-start.1
  1.9 1.0 %copy-done.1 = bf16[128,2048]{1,0:T(8,128)(2,1)S(1)} copy-done((bf16[128,2048]{1,0:T(8,128)(2,1)S(1)}, bf16[128,2048]{1,0:T(8,128)(2,1)}, u32[]{:S(2)}) %copy-start.1) | copy-done | bytes 524312
  2.9 0.0 copy-start.2
  2.9 1.0 %copy-done.2 = f32[2,512,128]{2,1,0:T(8,128)S(1)} copy-done((f32[2,512,128]{2,1,0:T(8,128)S(1)}, f32[2,512,128]{2,1,0:T(8,128)}, u32[]{:S(2)}) %copy-start.2) | copy-done | bytes 524312
  4.0 0.0 copy-start.3
  4.0 1.0 %copy-done.3 = bf16[256,1024]{1,0:T(8,128)(2,1)S(1)} copy-done((bf16[256,1024]{1,0:T(8,128)(2,1)S(1)}, bf16[256,1024]{1,0:T(8,128)(2,1)}, u32[]{:S(2)}) %copy-start.3) | copy-done | bytes 524312
  5.0 0.0 copy-start.4
  5.0 1.0 %copy-done.4 = bf16[1024,256]{1,0:T(8,128)(2,1)S(1)} copy-done((bf16[1024,256]{1,0:T(8,128)(2,1)S(1)}, bf16[1024,256]{1,0:T(8,128)(2,1)}, u32[]{:S(2)}) %copy-start.4) | copy-done | bytes 524312
  6.1 0.0 copy-start.5
  6.1 0.9 %copy-done.5 = bf16[256,256]{1,0:T(8,128)(2,1)S(1)} copy-done((bf16[256,256]{1,0:T(8,128)(2,1)S(1)}, bf16[256,256]{1,0:T(8,128)(2,1)}, u32[]{:S(2)}) %copy-start.5) | copy-done | bytes 131096
  7.0 0.0 copy-start.6
  7.0 0.9 %copy-done.6 = bf16[256,256]{1,0:T(8,128)(2,1)S(1)} copy-done((bf16[256,256]{1,0:T(8,128)(2,1)S(1)}, bf16[256,256]{1,0:T(8,128)(2,1)}, u32[]{:S(2)}) %copy-start.6) | copy-done | bytes 131096
  7.9 0.0 copy-start.7
  7.9 0.8 %copy-done.7 = bf16[128,256]{1,0:T(8,128)(2,1)S(1)} copy-done((bf16[128,256]{1,0:T(8,128)(2,1)S(1)}, bf16[128,256]{1,0:T(8,128)(2,1)}, u32[]{:S(2)}) %copy-start.7) | copy-done | bytes 65560
  8.7 0.0 copy-start.8
  8.7 0.7 %copy-done.8 = f32[3,3,256]{2,1,0:T(4,128)S(1)} copy-done((f32[3,3,256]{2,1,0:T(4,128)S(1)}, f32[3,3,256]{2,1,0:T(4,128)}, u32[]{:S(2)}) %copy-start.8) | copy-done | bytes 9240
  9.4 0.0 copy-start.9
  9.4 0.7 %copy-done.9 = f32[256]{0:T(256)S(1)} copy-done((f32[256]{0:T(256)S(1)}, f32[256]{0:T(256)}, u32[]{:S(2)}) %copy-start.9) | copy-done | bytes 1048
  10.1 39.9 %hyena.1 = bf16[128,256]{1,0:T(8,128)(2,1)S(1)} custom-call(bf16[128,2048]{1,0:T(8,128)(2,1)S(1)} %copy-done.1, bf16[3,2048,256]{2,1,0:T(8,128)(2,1)S(1)} %bitcast.2, f32[3,3,256]{2,1,0:T(4,128)S(1)} %copy-done.8, f32[1,256]{1,0:T(1,128)S(1)} %bitcast.3, bf16[128,256]{1,0:T(8,128)(2,1)S(1)} %copy-done.7, bf16[1024,256]{1,0:T(8,128)(2,1)S(1)} %copy-done.4, ...), custom_call_target="tpu_custom_call" | custom-call | tf_op jit(solution)/shard_map/hyena/pallas_call | solution.py:331
  50.0 0.6 %copy.12 = bf16[128,256]{1,0:T(8,128)(2,1)} copy(bf16[128,256]{1,0:T(8,128)(2,1)S(1)} %hyena.1) | data formatting | bytes 131072
Async XLA Ops:
  0.0 1.9 %copy-start = (bf16[2048,3,256]{2,0,1:T(8,128)(2,1)S(1)}, bf16[2048,3,256]{2,0,1:T(8,128)(2,1)}, u32[]{:S(2)}) copy-start(bf16[2048,3,256]{2,0,1:T(8,128)(2,1)} %param.11) | copy-start | bytes 9437188
  1.9 1.0 %copy-start.1 = (bf16[128,2048]{1,0:T(8,128)(2,1)S(1)}, bf16[128,2048]{1,0:T(8,128)(2,1)}, u32[]{:S(2)}) copy-start(bf16[128,2048]{1,0:T(8,128)(2,1)} %tokens.1) | copy-start | bytes 1572868
  2.9 1.0 %copy-start.2 = (f32[2,512,128]{2,1,0:T(8,128)S(1)}, f32[2,512,128]{2,1,0:T(8,128)}, u32[]{:S(2)}) copy-start(f32[2,512,128]{2,1,0:T(8,128)} %constant.14.clone.twist_h) | copy-start | bytes 1572868
  4.0 1.0 %copy-start.3 = (bf16[256,1024]{1,0:T(8,128)(2,1)S(1)}, bf16[256,1024]{1,0:T(8,128)(2,1)}, u32[]{:S(2)}) copy-start(bf16[256,1024]{1,0:T(8,128)(2,1)} %constant.11.clone.last_h) | copy-start | bytes 1572868
  5.0 1.0 %copy-start.4 = (bf16[1024,256]{1,0:T(8,128)(2,1)S(1)}, bf16[1024,256]{1,0:T(8,128)(2,1)}, u32[]{:S(2)}) copy-start(bf16[1024,256]{1,0:T(8,128)(2,1)} %constant.10.clone.first_h) | copy-start | bytes 1572868
  6.1 0.9 %copy-start.5 = (bf16[256,256]{1,0:T(8,128)(2,1)S(1)}, bf16[256,256]{1,0:T(8,128)(2,1)}, u32[]{:S(2)}) copy-start(bf16[256,256]{1,0:T(8,128)(2,1)} %constant.13.clone.behind_h) | copy-start | bytes 393220
  7.0 0.9 %copy-start.6 = (bf16[256,256]{1,0:T(8,128)(2,1)S(1)}, bf16[256,256]{1,0:T(8,128)(2,1)}, u32[]{:S(2)}) copy-start(bf16[256,256]{1,0:T(8,128)(2,1)} %constant.12.clone.ahead_h) | copy-start | bytes 393220
  7.9 0.8 %copy-start.7 = (bf16[128,256]{1,0:T(8,128)(2,1)S(1)}, bf16[128,256]{1,0:T(8,128)(2,1)}, u32[]{:S(2)}) copy-start(bf16[128,256]{1,0:T(8,128)(2,1)} %taps.1) | copy-start | bytes 196612
  8.7 0.7 %copy-start.8 = (f32[3,3,256]{2,1,0:T(4,128)S(1)}, f32[3,3,256]{2,1,0:T(4,128)}, u32[]{:S(2)}) copy-start(f32[3,3,256]{2,1,0:T(4,128)} %short.1) | copy-start | bytes 27652
  9.4 0.7 %copy-start.9 = (f32[256]{0:T(256)S(1)}, f32[256]{0:T(256)}, u32[]{:S(2)}) copy-start(f32[256]{0:T(256)} %param.13) | copy-start | bytes 3076

commit v2 on v1

--- a/solution.py
+++ b/solution.py
@@ -41,9 +41,9 @@
     sizes,
     tokens,
     weight,
-    short,
-    gain,
-    taps,
+    short_h,
+    gain_h,
+    taps_h,
     first_h,
     last_h,
     ahead_h,
@@ -56,6 +56,9 @@
     ahead,
     behind,
     twist,
+    short,
+    gain,
+    taps,
     held,
     acc,
     psend,
@@ -98,12 +101,15 @@
         pltpu.make_async_copy(source, target, load_sem.at[i])
         for i, (source, target) in enumerate(
             [
+                (taps_h, taps),
                 (weight, w),
                 (first_h, first),
+                (ahead_h, ahead),
+                (twist_h, twist),
                 (last_h, last),
-                (ahead_h, ahead),
                 (behind_h, behind),
-                (twist_h, twist),
+                (short_h, short),
+                (gain_h, gain),
             ]
         )
     ]
@@ -183,6 +189,7 @@
 
         lax.fori_loop(1, groups, go, 0)
 
+    loads[0].wait()
     tsend[...] = jnp.transpose(taps[...].astype(F32)).astype(BF16).reshape(groups, per, rows)
     exchange_start(0, tsend, trecv)
 
@@ -200,7 +207,6 @@
         load.wait()
     exchange_wait(0, tsend, trecv)
     tapspec[...] = spectrum(trecv[...].reshape(width, rows))
-    loads[0].wait()
 
     def part_copy(d):
         other = lax.rem(f + d, fsdp)
@@ -326,12 +332,12 @@
     made = tables(groups, per, rows)
     dma = pltpu.SemaphoreType.DMA
     vmem = pl.BlockSpec(memory_space=pltpu.VMEM)
-    anywhere = pl.BlockSpec(memory_space=pl.ANY)
+    hbm = pl.BlockSpec(memory_space=pl.ANY)
     half = 2 * groups * per
     return pl.pallas_call(
         functools.partial(kernel, sizes),
         out_shape=jax.ShapeDtypeStruct((rows, width), BF16),
-        in_specs=[anywhere, anywhere, vmem, vmem, vmem] + [anywhere] * 5,
+        in_specs=[hbm] * 10,
         out_specs=vmem,
         scratch_shapes=[
             pltpu.VMEM((branches, depth, width), BF16),
@@ -340,6 +346,9 @@
             pltpu.VMEM(made[2].shape, BF16),
             pltpu.VMEM(made[3].shape, BF16),
             pltpu.VMEM(made[4].shape, F32),
+            pltpu.VMEM(short_weight.shape, F32),
+            pltpu.VMEM((1, width), F32),
+            pltpu.VMEM((rows, width), BF16),
             pltpu.VMEM((fsdp, CHUNKS, rows, depth // CHUNKS), BF16),
             pltpu.VMEM((branches, rows, width), F32),
             pltpu.VMEM((fsdp - 1, branches, rows, width), BF16),
@@ -352,7 +361,7 @@
         + [pltpu.VMEM((groups, per, rows), BF16)] * 6
         + [
             pltpu.VMEM((half, 2 * rows), BF16),
-            dma((6,)),
+            dma((9,)),
             dma((fsdp, CHUNKS)),
             dma((fsdp, CHUNKS)),
             dma((fsdp - 1,)),
@@ -362,7 +371,7 @@
             dma((3, groups)),
         ],
         compiler_params=pltpu.CompilerParams(
-            collective_id=0, has_side_effects=True, vmem_limit_bytes=48 * 1024 * 1024
+            collective_id=0, has_side_effects=True, vmem_limit_bytes=60 * 1024 * 1024
         ),
         name="hyena",
     )(

time: 51.1 us -> 41.8 us (0.82)
  local copies, waits for them, and re-layouts: 10.7 us -> 1.47 us
    unnamed x21 -> x1, local copies, waits for them, and re-layouts: 10.7 us -> 1.47 us
where the time goes in v2:
time: 41.8 us; the launch traced here: 41.6 us
  Pallas kernels  40.2 us (96%)
  local copies, waits for them, and re-layouts  1.47 us (4%)
    pallas_call x1, Pallas kernels, per_device(): pl.pallas_call(functools.partial(kernel, sizes), out_shape=jax.ShapeDtype...  40.2 us
    unnamed x1, local copies, waits for them, and re-layouts  1.47 us

profile of v2, /device:TPU:0, one launch (start us, length us, event | category | flops | bytes accessed | tf_op | source)
XLA Modules:
  0.0 41.6 jit_solution(6355070495108482765)
XLA Ops:
  0.0 40.2 %hyena.1 = bf16[128,256]{1,0:T(8,128)(2,1)} custom-call(bf16[128,2048]{1,0:T(8,128)(2,1)} %tokens.1, bf16[3,2048,256]{2,1,0:T(8,128)(2,1)} %bitcast.2, f32[3,3,256]{2,1,0:T(4,128)} %short_h.1, f32[1,256]{1,0:T(1,128)} %bitcast.3, bf16[128,256]{1,0:T(8,128)(2,1)} %taps_h.1, bf16[1024,256]{1,0:T(8,128)(2,1)} %constant.10.clone.first_h, ...), custom_call_target="tpu_custom_call" | custom-call | tf_op jit(solution)/shard_map/hyena/pallas_call | solution.py:337
  40.2 1.5 %copy.12 = bf16[128,256]{1,0:T(8,128)(2,1)} copy(bf16[128,256]{1,0:T(8,128)(2,1)} %hyena.1) | data formatting | bytes 131072

commit v3 on v2

--- a/solution.py
+++ b/solution.py
@@ -63,7 +63,6 @@
     acc,
     psend,
     precv,
-    hsend,
     hrecv,
     query,
     product,
@@ -77,17 +76,19 @@
     load_sem,
     tok_send,
     tok_recv,
+    fwd_send,
     part_send,
     part_recv,
-    halo_sem,
+    halo_send,
+    halo_recv,
     a2a_send,
     a2a_recv,
 ):
     seq, fsdp, chan = sizes
     groups = seq * fsdp
     rows = tokens.shape[0]
-    depth = weight.shape[1]
-    width = weight.shape[2]
+    depth = weight.shape[1] * weight.shape[2]
+    width = weight.shape[3]
     per = width // groups
     bins = 2 * groups
     step = depth // CHUNKS
@@ -102,7 +103,7 @@
         for i, (source, target) in enumerate(
             [
                 (taps_h, taps),
-                (weight, w),
+                (weight.at[pl.ds(1, 2)], w.at[pl.ds(1, 2)]),
                 (first_h, first),
                 (ahead_h, ahead),
                 (twist_h, twist),
@@ -110,6 +111,7 @@
                 (behind_h, behind),
                 (short_h, short),
                 (gain_h, gain),
+                (weight.at[pl.ds(0, 1)], w.at[pl.ds(0, 1)]),
             ]
         )
     ]
@@ -133,33 +135,34 @@
     lax.fori_loop(1, everyone, greet, 0)
     pl.semaphore_wait(barrier, everyone - 1)
 
-    def token_copy(i, cc, k):
+    sibling = lax.rem(c + 1, chan)
+
+    def token_copy(i, k, same):
         return pltpu.make_async_remote_copy(
             src_ref=tokens.at[:, pl.ds(i * depth + k * step, step)],
             dst_ref=held.at[f, k],
-            send_sem=tok_send.at[i * chan + cc, k],
+            send_sem=tok_send.at[i, k],
             recv_sem=tok_recv.at[f, k],
-            device_id={"fsdp": c * share + i, "chan": cc},
-            device_id_type=MESH,
-        )
-
-    def own_copy(i, k):
-        return pltpu.make_async_copy(
-            tokens.at[:, pl.ds(i * depth + k * step, step)], held.at[f, k], tok_recv.at[f, k]
+            device_id={"fsdp": c * share + i, "chan": sibling if same else k % chan},
+            device_id_type=MESH,
         )
 
     for k in range(CHUNKS):
         for i in range(share):
-            for cc in range(chan):
-                is_self = jnp.logical_and(c * share + i == f, c == cc)
-
-                @pl.when(jnp.logical_not(is_self))
-                def _():
-                    token_copy(i, cc, k).start()
-
-                @pl.when(is_self)
-                def _():
-                    own_copy(i, k).start()
+            stays = c * share + i == f
+
+            @pl.when(jnp.logical_not(stays))
+            def _():
+                token_copy(i, k, False).start()
+
+            @pl.when(stays)
+            def _():
+                token_copy(i, k, True).start()
+                pltpu.make_async_copy(
+                    tokens.at[:, pl.ds(i * depth + k * step, step)],
+                    held.at[f, k],
+                    tok_recv.at[f, k],
+                ).start()
 
     def exchange_copy(which, source, target, k):
         other = lax.rem(me + k, groups)
@@ -203,89 +206,150 @@
         b = jnp.concatenate([real_b, imag_b], axis=1)
         return jnp.dot(b, ahead[...], preferred_element_type=F32).astype(BF16)
 
-    for load in loads[1:]:
+    def arrival(spot, k):
+        block = held.at[spot, k]
+        pltpu.make_async_copy(block, block, tok_recv.at[spot, k]).wait()
+
+    def forward_copy(d, t):
+        k = t * chan + c
+        block = held.at[lax.rem(f + d, fsdp), k]
+        return pltpu.make_async_remote_copy(
+            src_ref=block,
+            dst_ref=block,
+            send_sem=fwd_send.at[d - 1, t],
+            recv_sem=tok_recv.at[lax.rem(f + d, fsdp), k],
+            device_id={"chan": sibling},
+            device_id_type=MESH,
+        )
+
+    def part_copy(d, j):
+        return pltpu.make_async_remote_copy(
+            src_ref=psend.at[d - 1, j],
+            dst_ref=precv.at[d - 1, j],
+            send_sem=part_send.at[d - 1, j],
+            recv_sem=part_recv.at[d - 1, j],
+            device_id={"fsdp": lax.rem(f + d, fsdp)},
+            device_id_type=MESH,
+        )
+
+    phases = ((1, 2), (0, 1))
+
+    def halo_target(d):
+        return s * fsdp + lax.rem(f + d, fsdp) + 1
+
+    def halo_copy(d, phase):
+        target = jnp.minimum(halo_target(d), groups - 1)
+        start, count = phases[phase]
+        return pltpu.make_async_remote_copy(
+            src_ref=acc.at[d - 1, pl.ds(start, count), pl.ds(rows - 8, 8)],
+            dst_ref=hrecv.at[f, pl.ds(start, count)],
+            send_sem=halo_send.at[d - 1, phase],
+            recv_sem=halo_recv.at[f, phase],
+            device_id={"seq": target // fsdp, "fsdp": target % fsdp},
+            device_id_type=MESH,
+        )
+
+    def halo_remote(d):
+        target = halo_target(d)
+        return jnp.logical_and(target < groups, target != me)
+
+    def halo_start(d, phase):
+        @pl.when(halo_remote(d))
+        def _():
+            halo_copy(d, phase).start()
+
+        start, count = phases[phase]
+
+        @pl.when(halo_target(d) == me)
+        def _():
+            hrecv[f, start : start + count] = acc[d - 1, start : start + count, rows - 8 :]
+
+    def halo_wait(phase):
+        start, count = phases[phase]
+        for h in range(fsdp):
+            local = jnp.logical_and(f > 0, f == h)
+
+            @pl.when(jnp.logical_and(me > 0, jnp.logical_not(local)))
+            def _():
+                block = hrecv.at[h, pl.ds(start, count)]
+                pltpu.make_async_copy(block, block, halo_recv.at[h, phase]).wait()
+
+    @pl.when(me == 0)
+    def _():
+        hrecv[...] = jnp.zeros_like(hrecv)
+
+    loads[1].wait()
+    for k in range(CHUNKS):
+        arrival(f, k)
+        for j in (1, 2):
+            term = jnp.dot(held[f, k], w[j, k], preferred_element_type=F32)
+            acc[fsdp - 1, j] = term if k == 0 else acc[fsdp - 1, j] + term
+    halo_start(fsdp, 0)
+
+    for d in range(1, fsdp):
+        spot = lax.rem(f + d, fsdp)
+        for t in range(CHUNKS // chan):
+            for b in range(chan):
+                k = t * chan + lax.rem(c + b, chan)
+                arrival(spot, k)
+                if b == 0:
+                    forward_copy(d, t).start()
+                final = (t + 1) * chan == CHUNKS and b == chan - 1
+                for j in (1, 2):
+                    term = jnp.dot(held[spot, k], w[j, k], preferred_element_type=F32)
+                    if t > 0 or b > 0:
+                        term = acc[d - 1, j] + term
+                    acc[d - 1, j] = term
+                    if final:
+                        psend[d - 1, j] = term.astype(BF16)
+                        part_copy(d, j).start()
+        halo_start(d, 0)
+
+    for load in loads[2:]:
         load.wait()
     exchange_wait(0, tsend, trecv)
     tapspec[...] = spectrum(trecv[...].reshape(width, rows))
 
-    def part_copy(d):
-        other = lax.rem(f + d, fsdp)
-        return pltpu.make_async_remote_copy(
-            src_ref=psend.at[d - 1],
-            dst_ref=precv.at[d - 1],
-            send_sem=part_send.at[d - 1],
-            recv_sem=part_recv.at[d - 1],
-            device_id={"fsdp": other},
-            device_id_type=MESH,
-        )
-
-    for d in range(1, fsdp + 1):
-        spot = lax.rem(f + d, fsdp)
-        for k in range(CHUNKS):
-            pltpu.make_async_copy(held.at[spot, k], held.at[spot, k], tok_recv.at[spot, k]).wait()
-            block = held[spot, k]
-            for j in range(3):
-                term = jnp.dot(
-                    block, w[j, k * step : (k + 1) * step, :], preferred_element_type=F32
-                )
-                if k == 0:
-                    acc[j] = term
-                else:
-                    acc[j] += term
-        if d < fsdp:
-            psend[d - 1] = acc[...].astype(BF16)
-            part_copy(d).start()
-
-    for d in range(1, fsdp):
-        part_copy(d).wait_recv()
-    total = acc[...]
-    for d in range(1, fsdp):
-        total = total + precv[d - 1].astype(F32)
-    projected = total.astype(BF16).astype(F32)
-
-    following = jnp.minimum(me + 1, groups - 1)
-    halo = pltpu.make_async_remote_copy(
-        src_ref=hsend,
-        dst_ref=hrecv,
-        send_sem=halo_sem.at[0],
-        recv_sem=halo_sem.at[1],
-        device_id={"seq": following // fsdp, "fsdp": following % fsdp},
-        device_id_type=MESH,
-    )
-    hsend[...] = projected[:, rows - 8 :, :]
-
-    @pl.when(me < groups - 1)
-    def _():
-        halo.start()
-
-    @pl.when(me == 0)
-    def _():
-        hrecv[...] = jnp.zeros_like(hrecv)
-
-    @pl.when(me > 0)
-    def _():
-        halo.wait_recv()
-
     row_ids = lax.broadcasted_iota(jnp.int32, (rows, width), 0)
-    branches = []
-    for j in range(3):
-        now = projected[j]
-        before = hrecv[j, 7:8, :]
-        earlier = hrecv[j, 6:7, :]
+
+    def branch(j):
+        total = acc[fsdp - 1, j]
+        edge = hrecv[0, j]
+        for d in range(1, fsdp):
+            part_copy(d, j).wait_recv()
+            total = total + precv[d - 1, j].astype(F32)
+            edge = edge + hrecv[d, j]
+        now = total.astype(BF16).astype(F32)
+        edge = edge.astype(BF16).astype(F32)
+        before = edge[7:8]
+        earlier = edge[6:7]
         one = jnp.where(row_ids == 0, before, pltpu.roll(now, 1, 0))
         two = jnp.where(
             row_ids == 0, earlier, jnp.where(row_ids == 1, before, pltpu.roll(now, 2, 0))
         )
-        branches.append(
+        return (
             short[0, j : j + 1, :] * now
             + short[1, j : j + 1, :] * one
             + short[2, j : j + 1, :] * two
         )
-    prod = (branches[1] * branches[2]).astype(BF16).astype(F32)
+
+    halo_wait(0)
+    prod = (branch(1) * branch(2)).astype(BF16).astype(F32)
     gsend[...] = jnp.transpose(prod).astype(BF16).reshape(groups, per, rows)
     exchange_start(1, gsend, grecv)
-    query[...] = branches[0]
     product[...] = prod * gain[...]
+
+    for d in range(1, fsdp + 1):
+        spot = lax.rem(f + d, fsdp)
+        term = jnp.dot(held[spot, 0], w[0, 0], preferred_element_type=F32)
+        for k in range(1, CHUNKS):
+            term += jnp.dot(held[spot, k], w[0, k], preferred_element_type=F32)
+        acc[d - 1, 0] = term
+        if d < fsdp:
+            psend[d - 1, 0] = term.astype(BF16)
+            part_copy(d, 0).start()
+        halo_start(d, 1)
+
     exchange_wait(1, gsend, grecv)
 
     x = spectrum(grecv[...].reshape(width, rows)).astype(F32)
@@ -303,24 +367,27 @@
     y = jnp.dot(last[...], packed, preferred_element_type=F32) * (1.0 / (bins * rows))
     csend[...] = y.astype(BF16).reshape(groups, per, rows)
     exchange_start(2, csend, crecv)
+    halo_wait(1)
+    query[...] = branch(0)
     exchange_wait(2, csend, crecv)
     conv = jnp.transpose(crecv[...].reshape(width, rows).astype(F32))
     out[...] = (query[...] * (conv + product[...])).astype(BF16)
 
-    @pl.when(me < groups - 1)
-    def _():
-        halo.wait_send()
+    for d in range(1, fsdp + 1):
+        for phase in range(2):
+
+            @pl.when(halo_remote(d))
+            def _():
+                halo_copy(d, phase).wait_send()
 
     for d in range(1, fsdp):
-        part_copy(d).wait_send()
+        for j in range(3):
+            part_copy(d, j).wait_send()
+        for t in range(CHUNKS // chan):
+            forward_copy(d, t).wait_send()
     for k in range(CHUNKS):
         for i in range(share):
-            for cc in range(chan):
-                is_self = jnp.logical_and(c * share + i == f, c == cc)
-
-                @pl.when(jnp.logical_not(is_self))
-                def _():
-                    token_copy(i, cc, k).wait_send()
+            token_copy(i, k, False).wait_send()
 
 
 def per_device(sizes, tokens, proj_weight, short_weight, skip_gain, filter_taps):
@@ -340,7 +407,7 @@
         in_specs=[hbm] * 10,
         out_specs=vmem,
         scratch_shapes=[
-            pltpu.VMEM((branches, depth, width), BF16),
+            pltpu.VMEM((branches, CHUNKS, depth // CHUNKS, width), BF16),
             pltpu.VMEM(made[0].shape, BF16),
             pltpu.VMEM(made[1].shape, BF16),
             pltpu.VMEM(made[2].shape, BF16),
@@ -350,23 +417,24 @@
             pltpu.VMEM((1, width), F32),
             pltpu.VMEM((rows, width), BF16),
             pltpu.VMEM((fsdp, CHUNKS, rows, depth // CHUNKS), BF16),
-            pltpu.VMEM((branches, rows, width), F32),
+            pltpu.VMEM((fsdp, branches, rows, width), F32),
             pltpu.VMEM((fsdp - 1, branches, rows, width), BF16),
             pltpu.VMEM((fsdp - 1, branches, rows, width), BF16),
-            pltpu.VMEM((branches, 8, width), F32),
-            pltpu.VMEM((branches, 8, width), F32),
+            pltpu.VMEM((fsdp, branches, 8, width), F32),
             pltpu.VMEM((rows, width), F32),
             pltpu.VMEM((rows, width), F32),
         ]
         + [pltpu.VMEM((groups, per, rows), BF16)] * 6
         + [
             pltpu.VMEM((half, 2 * rows), BF16),
-            dma((9,)),
+            dma((10,)),
+            dma((fsdp // chan, CHUNKS)),
             dma((fsdp, CHUNKS)),
-            dma((fsdp, CHUNKS)),
-            dma((fsdp - 1,)),
-            dma((fsdp - 1,)),
-            dma((2,)),
+            dma((fsdp - 1, CHUNKS // chan)),
+            dma((fsdp - 1, branches)),
+            dma((fsdp - 1, branches)),
+            dma((fsdp, 2)),
+            dma((fsdp, 2)),
             dma((3, groups)),
             dma((3, groups)),
         ],
@@ -376,7 +444,7 @@
         name="hyena",
     )(
         tokens,
-        jnp.transpose(proj_weight, (1, 0, 2)),
+        jnp.transpose(proj_weight, (1, 0, 2)).reshape(branches, CHUNKS, depth // CHUNKS, width),
         short_weight,
         skip_gain.reshape(1, width),
         filter_taps,

time: 41.8 us -> 32.4 us (0.78)
  Pallas kernels: 40.2 us -> 30.7 us
    pallas_call x1, Pallas kernels: 40.2 us -> 30.7 us  [per_device(): pl.pallas_call(functools.partial(kernel, sizes), out_shape=jax.ShapeDtype...]
where the time goes in v3:
time: 32.4 us; the launch traced here: 32.2 us
  Pallas kernels  30.7 us (95%)
  local copies, waits for them, and re-layouts  1.47 us (5%)
    pallas_call x1, Pallas kernels, per_device(): pl.pallas_call(functools.partial(kernel, sizes), out_shape=jax.ShapeDtype...  30.7 us
    unnamed x1, local copies, waits for them, and re-layouts  1.47 us

profile of v3, /device:TPU:0, one launch (start us, length us, event | category | flops | bytes accessed | tf_op | source)
XLA Modules:
  0.0 32.2 jit_solution(12756088307002773813)
XLA Ops:
  0.0 30.7 %hyena.1 = bf16[128,256]{1,0:T(8,128)(2,1)} custom-call(bf16[128,2048]{1,0:T(8,128)(2,1)} %tokens.1, bf16[3,4,512,256]{3,2,1,0:T(8,128)(2,1)} %bitcast.4, f32[3,3,256]{2,1,0:T(4,128)} %short_h.1, f32[1,256]{1,0:T(1,128)} %bitcast.5, bf16[128,256]{1,0:T(8,128)(2,1)} %taps_h.1, bf16[1024,256]{1,0:T(8,128)(2,1)} %constant.10.clone.first_h, ...), custom_call_target="tpu_custom_call" | custom-call | tf_op jit(solution)/shard_map/hyena/pallas_call | solution.py:404
  30.7 1.5 %copy.12 = bf16[128,256]{1,0:T(8,128)(2,1)} copy(bf16[128,256]{1,0:T(8,128)(2,1)} %hyena.1) | data formatting | bytes 131072

commit v4 on v3

--- a/solution.py
+++ b/solution.py
@@ -13,7 +13,8 @@
 MESH = pl.DeviceIdType.MESH
 BF16 = jnp.bfloat16
 F32 = jnp.float32
-CHUNKS = 4
+MOST_CHUNKS = 2
+HALVES = 2
 
 
 def phase_pair(rows, cols, period):
@@ -87,11 +88,13 @@
     seq, fsdp, chan = sizes
     groups = seq * fsdp
     rows = tokens.shape[0]
-    depth = weight.shape[1] * weight.shape[2]
+    chunks = weight.shape[1]
+    lines = rows // HALVES
+    depth = chunks * weight.shape[2]
     width = weight.shape[3]
     per = width // groups
     bins = 2 * groups
-    step = depth // CHUNKS
+    step = depth // chunks
     share = fsdp // chan
     s = lax.axis_index("seq")
     f = lax.axis_index("fsdp")
@@ -132,36 +135,46 @@
         )
         return carry
 
-    lax.fori_loop(1, everyone, greet, 0)
+    lax.fori_loop(1, everyone, greet, 0, unroll=everyone <= 16)
+
+    @pl.when(me == 0)
+    def _():
+        hrecv[...] = jnp.zeros_like(hrecv)
+
+    loads[0].wait()
+    tsend[...] = jnp.transpose(taps[...].astype(F32)).astype(BF16).reshape(groups, per, rows)
     pl.semaphore_wait(barrier, everyone - 1)
 
     sibling = lax.rem(c + 1, chan)
 
-    def token_copy(i, k, same):
+    def span(h):
+        return pl.ds(h * lines, lines)
+
+    def token_copy(i, h, k, same):
         return pltpu.make_async_remote_copy(
-            src_ref=tokens.at[:, pl.ds(i * depth + k * step, step)],
-            dst_ref=held.at[f, k],
-            send_sem=tok_send.at[i, k],
-            recv_sem=tok_recv.at[f, k],
+            src_ref=tokens.at[span(h), pl.ds(i * depth + k * step, step)],
+            dst_ref=held.at[f, k, span(h)],
+            send_sem=tok_send.at[i, h, k],
+            recv_sem=tok_recv.at[f, h, k],
             device_id={"fsdp": c * share + i, "chan": sibling if same else k % chan},
             device_id_type=MESH,
         )
 
-    for k in range(CHUNKS):
+    for h, k in [(h, k) for h in range(HALVES) for k in range(chunks)]:
         for i in range(share):
             stays = c * share + i == f
 
             @pl.when(jnp.logical_not(stays))
             def _():
-                token_copy(i, k, False).start()
+                token_copy(i, h, k, False).start()
 
             @pl.when(stays)
             def _():
-                token_copy(i, k, True).start()
+                token_copy(i, h, k, True).start()
                 pltpu.make_async_copy(
-                    tokens.at[:, pl.ds(i * depth + k * step, step)],
-                    held.at[f, k],
-                    tok_recv.at[f, k],
+                    tokens.at[span(h), pl.ds(i * depth + k * step, step)],
+                    held.at[f, k, span(h)],
+                    tok_recv.at[f, h, k],
                 ).start()
 
     def exchange_copy(which, source, target, k):
@@ -180,20 +193,23 @@
             exchange_copy(which, source, target, k).start()
             return carry
 
-        lax.fori_loop(1, groups, go, 0)
+        lax.fori_loop(1, groups, go, 0, unroll=groups <= 8)
         target[me] = source[me]
 
     def exchange_wait(which, source, target):
         def go(k, carry):
-            copy = exchange_copy(which, source, target, k)
-            copy.wait_send()
-            copy.wait_recv()
+            exchange_copy(which, source, target, k).wait_recv()
             return carry
 
+        lax.fori_loop(1, groups, go, 0, unroll=groups <= 8)
+
+    def exchange_sent(which, source, target):
+        def go(k, carry):
+            exchange_copy(which, source, target, k).wait_send()
+            return carry
+
         lax.fori_loop(1, groups, go, 0)
 
-    loads[0].wait()
-    tsend[...] = jnp.transpose(taps[...].astype(F32)).astype(BF16).reshape(groups, per, rows)
     exchange_start(0, tsend, trecv)
 
     half = bins * per
@@ -206,28 +222,28 @@
         b = jnp.concatenate([real_b, imag_b], axis=1)
         return jnp.dot(b, ahead[...], preferred_element_type=F32).astype(BF16)
 
-    def arrival(spot, k):
-        block = held.at[spot, k]
-        pltpu.make_async_copy(block, block, tok_recv.at[spot, k]).wait()
-
-    def forward_copy(d, t):
+    def arrival(spot, h, k):
+        block = held.at[spot, k, span(h)]
+        pltpu.make_async_copy(block, block, tok_recv.at[spot, h, k]).wait()
+
+    def forward_copy(d, h, t):
         k = t * chan + c
-        block = held.at[lax.rem(f + d, fsdp), k]
+        block = held.at[lax.rem(f + d, fsdp), k, span(h)]
         return pltpu.make_async_remote_copy(
             src_ref=block,
             dst_ref=block,
-            send_sem=fwd_send.at[d - 1, t],
-            recv_sem=tok_recv.at[lax.rem(f + d, fsdp), k],
+            send_sem=fwd_send.at[d - 1, h, t],
+            recv_sem=tok_recv.at[lax.rem(f + d, fsdp), h, k],
             device_id={"chan": sibling},
             device_id_type=MESH,
         )
 
-    def part_copy(d, j):
+    def part_copy(d, j, h):
         return pltpu.make_async_remote_copy(
-            src_ref=psend.at[d - 1, j],
-            dst_ref=precv.at[d - 1, j],
-            send_sem=part_send.at[d - 1, j],
-            recv_sem=part_recv.at[d - 1, j],
+            src_ref=psend.at[d - 1, j, span(h)],
+            dst_ref=precv.at[d - 1, j, span(h)],
+            send_sem=part_send.at[d - 1, j, h],
+            recv_sem=part_recv.at[d - 1, j, h],
             device_id={"fsdp": lax.rem(f + d, fsdp)},
             device_id_type=MESH,
         )
@@ -274,13 +290,10 @@
                 block = hrecv.at[h, pl.ds(start, count)]
                 pltpu.make_async_copy(block, block, halo_recv.at[h, phase]).wait()
 
-    @pl.when(me == 0)
-    def _():
-        hrecv[...] = jnp.zeros_like(hrecv)
-
     loads[1].wait()
-    for k in range(CHUNKS):
-        arrival(f, k)
+    for k in range(chunks):
+        for h in range(HALVES):
+            arrival(f, h, k)
         for j in (1, 2):
             term = jnp.dot(held[f, k], w[j, k], preferred_element_type=F32)
             acc[fsdp - 1, j] = term if k == 0 else acc[fsdp - 1, j] + term
@@ -288,21 +301,26 @@
 
     for d in range(1, fsdp):
         spot = lax.rem(f + d, fsdp)
-        for t in range(CHUNKS // chan):
-            for b in range(chan):
-                k = t * chan + lax.rem(c + b, chan)
-                arrival(spot, k)
-                if b == 0:
-                    forward_copy(d, t).start()
-                final = (t + 1) * chan == CHUNKS and b == chan - 1
-                for j in (1, 2):
-                    term = jnp.dot(held[spot, k], w[j, k], preferred_element_type=F32)
-                    if t > 0 or b > 0:
-                        term = acc[d - 1, j] + term
-                    acc[d - 1, j] = term
-                    if final:
-                        psend[d - 1, j] = term.astype(BF16)
-                        part_copy(d, j).start()
+        for h, t, b in [
+            (h, t, b)
+            for h in range(HALVES)
+            for t in range(chunks // chan)
+            for b in range(chan)
+        ]:
+            k = t * chan + lax.rem(c + b, chan)
+            arrival(spot, h, k)
+            if b == 0:
+                forward_copy(d, h, t).start()
+            final = (t + 1) * chan == chunks and b == chan - 1
+            at = slice(h * lines, (h + 1) * lines)
+            for j in (1, 2):
+                term = jnp.dot(held[spot, k, at], w[j, k], preferred_element_type=F32)
+                if t > 0 or b > 0:
+                    term = acc[d - 1, j, at] + term
+                acc[d - 1, j, at] = term
+                if final:
+                    psend[d - 1, j, at] = term.astype(BF16)
+                    part_copy(d, j, h).start()
         halo_start(d, 0)
 
     for load in loads[2:]:
@@ -316,7 +334,8 @@
         total = acc[fsdp - 1, j]
         edge = hrecv[0, j]
         for d in range(1, fsdp):
-            part_copy(d, j).wait_recv()
+            for h in range(HALVES):
+                part_copy(d, j, h).wait_recv()
             total = total + precv[d - 1, j].astype(F32)
             edge = edge + hrecv[d, j]
         now = total.astype(BF16).astype(F32)
@@ -342,12 +361,13 @@
     for d in range(1, fsdp + 1):
         spot = lax.rem(f + d, fsdp)
         term = jnp.dot(held[spot, 0], w[0, 0], preferred_element_type=F32)
-        for k in range(1, CHUNKS):
+        for k in range(1, chunks):
             term += jnp.dot(held[spot, k], w[0, k], preferred_element_type=F32)
         acc[d - 1, 0] = term
         if d < fsdp:
             psend[d - 1, 0] = term.astype(BF16)
-            part_copy(d, 0).start()
+            for h in range(HALVES):
+                part_copy(d, 0, h).start()
         halo_start(d, 1)
 
     exchange_wait(1, gsend, grecv)
@@ -373,6 +393,9 @@
     conv = jnp.transpose(crecv[...].reshape(width, rows).astype(F32))
     out[...] = (query[...] * (conv + product[...])).astype(BF16)
 
+    exchange_sent(0, tsend, trecv)
+    exchange_sent(1, gsend, grecv)
+    exchange_sent(2, csend, crecv)
     for d in range(1, fsdp + 1):
         for phase in range(2):
 
@@ -381,13 +404,14 @@
                 halo_copy(d, phase).wait_send()
 
     for d in range(1, fsdp):
-        for j in range(3):
-            part_copy(d, j).wait_send()
-        for t in range(CHUNKS // chan):
-            forward_copy(d, t).wait_send()
-    for k in range(CHUNKS):
+        for h in range(HALVES):
+            for j in range(3):
+                part_copy(d, j, h).wait_send()
+            for t in range(chunks // chan):
+                forward_copy(d, h, t).wait_send()
+    for h, k in [(h, k) for h in range(HALVES) for k in range(chunks)]:
         for i in range(share):
-            token_copy(i, k, False).wait_send()
+            token_copy(i, h, k, False).wait_send()
 
 
 def per_device(sizes, tokens, proj_weight, short_weight, skip_gain, filter_taps):
@@ -396,6 +420,7 @@
     rows = tokens.shape[0]
     depth, branches, width = proj_weight.shape
     per = width // groups
+    chunks = min(MOST_CHUNKS, depth // 128)
     made = tables(groups, per, rows)
     dma = pltpu.SemaphoreType.DMA
     vmem = pl.BlockSpec(memory_space=pltpu.VMEM)
@@ -407,7 +432,7 @@
         in_specs=[hbm] * 10,
         out_specs=vmem,
         scratch_shapes=[
-            pltpu.VMEM((branches, CHUNKS, depth // CHUNKS, width), BF16),
+            pltpu.VMEM((branches, chunks, depth // chunks, width), BF16),
             pltpu.VMEM(made[0].shape, BF16),
             pltpu.VMEM(made[1].shape, BF16),
             pltpu.VMEM(made[2].shape, BF16),
@@ -416,7 +441,7 @@
             pltpu.VMEM(short_weight.shape, F32),
             pltpu.VMEM((1, width), F32),
             pltpu.VMEM((rows, width), BF16),
-            pltpu.VMEM((fsdp, CHUNKS, rows, depth // CHUNKS), BF16),
+            pltpu.VMEM((fsdp, chunks, rows, depth // chunks), BF16),
             pltpu.VMEM((fsdp, branches, rows, width), F32),
             pltpu.VMEM((fsdp - 1, branches, rows, width), BF16),
             pltpu.VMEM((fsdp - 1, branches, rows, width), BF16),
@@ -428,11 +453,11 @@
         + [
             pltpu.VMEM((half, 2 * rows), BF16),
             dma((10,)),
-            dma((fsdp // chan, CHUNKS)),
-            dma((fsdp, CHUNKS)),
-            dma((fsdp - 1, CHUNKS // chan)),
-            dma((fsdp - 1, branches)),
-            dma((fsdp - 1, branches)),
+            dma((fsdp // chan, HALVES, chunks)),
+            dma((fsdp, HALVES, chunks)),
+            dma((fsdp - 1, HALVES, chunks // chan)),
+            dma((fsdp - 1, branches, HALVES)),
+            dma((fsdp - 1, branches, HALVES)),
             dma((fsdp, 2)),
             dma((fsdp, 2)),
             dma((3, groups)),
@@ -444,7 +469,7 @@
         name="hyena",
     )(
         tokens,
-        jnp.transpose(proj_weight, (1, 0, 2)).reshape(branches, CHUNKS, depth // CHUNKS, width),
+        jnp.transpose(proj_weight, (1, 0, 2)).reshape(branches, chunks, depth // chunks, width),
         short_weight,
         skip_gain.reshape(1, width),
         filter_taps,

time: 32.4 us -> 31.7 us (0.978)
  Pallas kernels: 30.7 us -> 30.1 us
    pallas_call x1, Pallas kernels: 30.7 us -> 30.1 us  [per_device(): pl.pallas_call(functools.partial(kernel, sizes), out_shape=jax.ShapeDtype...]
where the time goes in v4:
time: 31.7 us; the launch traced here: 31.6 us
  Pallas kernels  30.1 us (95%)
  local copies, waits for them, and re-layouts  1.47 us (5%)
    pallas_call x1, Pallas kernels, per_device(): pl.pallas_call(functools.partial(kernel, sizes), out_shape=jax.ShapeDtype...  30.1 us
    unnamed x1, local copies, waits for them, and re-layouts  1.47 us

profile of v4, /device:TPU:0, one launch (start us, length us, event | category | flops | bytes accessed | tf_op | source)
XLA Modules:
  0.0 31.6 jit_solution(2525107259832828087)
XLA Ops:
  0.0 30.1 %hyena.1 = bf16[128,256]{1,0:T(8,128)(2,1)} custom-call(bf16[128,2048]{1,0:T(8,128)(2,1)} %tokens.1, bf16[3,2,1024,256]{3,2,1,0:T(8,128)(2,1)} %bitcast.4, f32[3,3,256]{2,1,0:T(4,128)} %short_h.1, f32[1,256]{1,0:T(1,128)} %bitcast.5, bf16[128,256]{1,0:T(8,128)(2,1)} %taps_h.1, bf16[1024,256]{1,0:T(8,128)(2,1)} %constant.10.clone.first_h, ...), custom_call_target="tpu_custom_call" | custom-call | tf_op jit(solution)/shard_map/hyena/pallas_call | solution.py:429
  30.1 1.5 %copy.12 = bf16[128,256]{1,0:T(8,128)(2,1)} copy(bf16[128,256]{1,0:T(8,128)(2,1)} %hyena.1) | data formatting | bytes 131072

commit v5 on v4

--- a/solution.py
+++ b/solution.py
@@ -210,7 +210,6 @@
 
         lax.fori_loop(1, groups, go, 0)
 
-    exchange_start(0, tsend, trecv)
 
     half = bins * per
 
@@ -325,8 +324,7 @@
 
     for load in loads[2:]:
         load.wait()
-    exchange_wait(0, tsend, trecv)
-    tapspec[...] = spectrum(trecv[...].reshape(width, rows))
+    exchange_start(0, tsend, trecv)
 
     row_ids = lax.broadcasted_iota(jnp.int32, (rows, width), 0)
 
@@ -366,11 +364,15 @@
         acc[d - 1, 0] = term
         if d < fsdp:
             psend[d - 1, 0] = term.astype(BF16)
+
+    exchange_wait(0, tsend, trecv)
+    tapspec[...] = spectrum(trecv[...].reshape(width, rows))
+    exchange_wait(1, gsend, grecv)
+    for d in range(1, fsdp + 1):
+        if d < fsdp:
             for h in range(HALVES):
                 part_copy(d, 0, h).start()
         halo_start(d, 1)
-
-    exchange_wait(1, gsend, grecv)
 
     x = spectrum(grecv[...].reshape(width, rows)).astype(F32)
     t = tapspec[...].astype(F32)

time: 31.7 us -> 31.6 us (level)
  no operation moved by 1% of the time
where the time goes in v5:
time: 31.6 us; the launch traced here: 31.4 us
  Pallas kernels  29.9 us (95%)
  local copies, waits for them, and re-layouts  1.47 us (5%)
    pallas_call x1, Pallas kernels, per_device(): pl.pallas_call(functools.partial(kernel, sizes), out_shape=jax.ShapeDtype...  29.9 us
    unnamed x1, local copies, waits for them, and re-layouts  1.47 us

profile of v5, /device:TPU:0, one launch (start us, length us, event | category | flops | bytes accessed | tf_op | source)
XLA Modules:
  0.0 31.4 jit_solution(8321530515205569670)
XLA Ops:
  0.0 29.9 %hyena.1 = bf16[128,256]{1,0:T(8,128)(2,1)} custom-call(bf16[128,2048]{1,0:T(8,128)(2,1)} %tokens.1, bf16[3,2,1024,256]{3,2,1,0:T(8,128)(2,1)} %bitcast.4, f32[3,3,256]{2,1,0:T(4,128)} %short_h.1, f32[1,256]{1,0:T(1,128)} %bitcast.5, bf16[128,256]{1,0:T(8,128)(2,1)} %taps_h.1, bf16[1024,256]{1,0:T(8,128)(2,1)} %constant.10.clone.first_h, ...), custom_call_target="tpu_custom_call" | custom-call | tf_op jit(solution)/shard_map/hyena/pallas_call | solution.py:431
  29.9 1.5 %copy.12 = bf16[128,256]{1,0:T(8,128)(2,1)} copy(bf16[128,256]{1,0:T(8,128)(2,1)} %hyena.1) | data formatting | bytes 131072
